TPU v7x, 32 devices: a whole 2x2x4 slice. The times are simulated.
32 devices in a mesh: ctx: 8 (over z, x), head: 2 (over y), dp: 2 (over core).
Axes of the slice: x: 2, y: 2, z: 4, core: 2. Of those that a mesh axis runs over, the one named last changes fastest.
Arguments:
- queries: bfloat16 [2, 2048, 32, 128], P('dp', 'ctx', 'head'), may hold values from -7 to 7
- keys: bfloat16 [2, 2048, 16, 128], P('dp', 'ctx', 'head'), may hold values from -7 to 7
- values: bfloat16 [2, 2048, 16, 128], P('dp', 'ctx', 'head'), may hold values from -6 to 6
- d_out: bfloat16 [2, 2048, 32, 128], P('dp', 'ctx', 'head'), may hold values from -6 to 6
- loss_mask: int32 [2, 2048], P('dp', 'ctx'), may hold values from 0 to 1, as said below
- turn_ids: int32 [2, 2048], P('dp', 'ctx'), may hold values from 0 to 1, never falling along the last dimension, each value on 1 to 1536 neighbouring positions
Outputs:
- d_queries: bfloat16 [2, 2048, 32, 128], P('dp', 'ctx', 'head')
- d_keys: bfloat16 [2, 2048, 16, 128], P('dp', 'ctx', 'head')
- d_values: bfloat16 [2, 2048, 16, 128], P('dp', 'ctx', 'head')
Inputs may be any that keep to these rules, and one draw needn't show every extreme that they name: `loss_mask`: within each trajectory the share of ones grows with the position; position 0 of every trajectory is 1. `turn_ids`: turn ids never fall along a trajectory; each turn holds 1 to 1536 positions.
All inputs are finite; a program needn't handle non-finite values.
Results may differ from a plain program's by a relative error of at most 0.015.
Values may be sent and summed in bfloat16 or wider, within the bound.
A program may use at most 128 MiB of HBM per device.

v0:
```python
import jax
import jax.numpy as jnp
from jax import lax
from jax.sharding import PartitionSpec as P

WINDOW = 1024


SCALE = 168.0 ** (-0.5)


def from_behind(shard, axis, by):
    count = lax.axis_size(axis)
    pairs = [(i, i + by) for i in range(count) if 0 <= i + by < count]
    return lax.ppermute(shard, axis, pairs)


def group_scores(query_group, key_block, allowed):
    logits = (
        jnp.einsum("tgd,jd->gtj", query_group, key_block, preferred_element_type=jnp.float32)
        * SCALE
    )
    return jnp.where(allowed[None], logits, -jnp.inf)


def group_grads(prob_f32, grad_group, value_block, deltas):
    grad_probs = jnp.einsum(
        "tgd,jd->gtj", grad_group, value_block, preferred_element_type=jnp.float32
    )
    return (prob_f32 * (grad_probs - deltas[:, :, None]) * SCALE).astype(jnp.bfloat16)


def on_device(queries, keys, values, d_out, loss_mask, turn_ids):
    rows_dev = queries.shape[1]
    heads_q = queries.shape[2]
    heads_kv = keys.shape[2]
    group_size = heads_q // heads_kv
    hop_total = WINDOW // rows_dev
    key_span = WINDOW + rows_dev
    count_all = lax.psum(jnp.sum(loss_mask).astype(jnp.float32), ("ctx", "dp"))
    factor = rows_dev * lax.axis_size("ctx") * lax.axis_size("dp") / count_all
    query_local = queries[0]
    grad_local = d_out[0] * loss_mask[0][:, None, None].astype(jnp.bfloat16)
    key_local = keys[0]
    value_local = values[0]
    turn_marks = (turn_ids[0] + 1).astype(jnp.bfloat16)
    key_parts = []
    value_parts = []
    mark_parts = []
    for distance in range(hop_total, 0, -1):
        far_keys, far_values, far_marks = from_behind(
            (key_local, value_local, turn_marks), "ctx", distance
        )
        key_parts.append(far_keys)
        value_parts.append(far_values)
        mark_parts.append(far_marks)
    key_ext = jnp.concatenate(key_parts + [key_local], axis=0)
    value_ext = jnp.concatenate(value_parts + [value_local], axis=0)
    mark_ext = jnp.concatenate(mark_parts + [turn_marks], axis=0)
    row_index = lax.broadcasted_iota(jnp.int32, (rows_dev, key_span), 0)
    col_index = lax.broadcasted_iota(jnp.int32, (rows_dev, key_span), 1)
    allowed = (
        (col_index > row_index)
        & (col_index <= row_index + WINDOW)
        & (mark_ext[None, :] == turn_marks[:, None])
    )
    first_col = 0
    query_grads = []
    key_grads = []
    value_grads = []
    top_parts = []
    total_parts = []
    delta_parts = []
    for group in range(heads_kv):
        low_head = group * group_size
        query_group = query_local[:, low_head : low_head + group_size, :]
        grad_group = grad_local[:, low_head : low_head + group_size, :]
        key_block = key_ext[:, group, :]
        value_block = value_ext[:, group, :]
        logits = group_scores(query_group, key_block, allowed)
        top_score = jnp.max(logits, axis=2)
        raised = jnp.exp(logits - top_score[:, :, None])
        totals = jnp.sum(raised, axis=2)
        prob_f32 = raised / totals[:, :, None]
        prob_b16 = prob_f32.astype(jnp.bfloat16)
        outputs = jnp.einsum(
            "gtj,jd->tgd", prob_b16, value_block, preferred_element_type=jnp.float32
        ).astype(jnp.bfloat16)
        deltas = jnp.transpose(
            jnp.sum(grad_group.astype(jnp.float32) * outputs.astype(jnp.float32), axis=2)
        )
        grad_logits = group_grads(prob_f32, grad_group, value_block, deltas)
        query_grads.append(
            jnp.einsum("gtj,jd->tgd", grad_logits, key_block, preferred_element_type=jnp.float32)
        )
        key_grads.append(
            jnp.einsum("gtj,tgd->jd", grad_logits, query_group, preferred_element_type=jnp.float32)
        )
        value_grads.append(
            jnp.einsum("gtj,tgd->jd", prob_b16, grad_group, preferred_element_type=jnp.float32)
        )
        top_parts.append(jnp.transpose(top_score))
        total_parts.append(jnp.transpose(totals))
        delta_parts.append(jnp.transpose(deltas))
    grad_query = jnp.concatenate(query_grads, axis=1)
    key_acc = jnp.stack(key_grads, axis=1)
    value_acc = jnp.stack(value_grads, axis=1)
    key_own = key_acc[WINDOW:]
    value_own = value_acc[WINDOW:]
    for distance in range(1, hop_total + 1):
        low_row = (hop_total - distance) * rows_dev
        back_key, back_value = from_behind(
            (key_acc[low_row : low_row + rows_dev], value_acc[low_row : low_row + rows_dev]),
            "ctx",
            -distance,
        )
        key_own = key_own + back_key
        value_own = value_own + back_value
    d_queries = (grad_query * factor).astype(jnp.bfloat16)[None]
    d_keys = (key_own * factor).astype(jnp.bfloat16)[None]
    d_values = (value_own * factor).astype(jnp.bfloat16)[None]
    return (d_queries, d_keys, d_values)


def solution(mesh):
    return jax.shard_map(
        on_device,
        mesh=mesh,
        in_specs=(
            P("dp", "ctx", "head", None),
            P("dp", "ctx", "head", None),
            P("dp", "ctx", "head", None),
            P("dp", "ctx", "head", None),
            P("dp", "ctx"),
            P("dp", "ctx"),
        ),
        out_specs=(
            P("dp", "ctx", "head", None),
            P("dp", "ctx", "head", None),
            P("dp", "ctx", "head", None),
        ),
        check_vma=False,
    )
```

profile of v0, /device:TPU:8, one launch (start us, length us, event | category | flops | bytes accessed | tf_op | source)
XLA Modules:
  0.0 527.4 jit_solution(16742124187261356483)
XLA Ops:
  4.8 3.5 collective-permute-start.6
  21.4 25.0 %psum.7 = f32[]{:T(128)} all-reduce(f32[]{:T(128)S(6)} %convert_element_type.244), channel_id=1, replica_groups=mesh['ctx'=8,'head'=2,'dp'=2] {'ctx','dp'}, use_global_device_ids=true, to_apply=%region_25.26 | all-reduce | flops 1 | bytes 8 | tf_op jit(solution)/shard_map/psum | solution.py:40
  52.0 9.3 %collective-permute-start.1 = (bf16[256,8,128]{2,0,1:T(8,128)(2,1)}, bf16[256,8,128]{2,0,1:T(8,128)(2,1)}, u32[]{:S(2)}, u32[]{:S(2)}) collective-permute-start(bf16[256,8,128]{2,0,1:T(8,128)(2,1)} %bitcast.666), channel_id=1, source_target_pairs={{0,12},{4,16},{8,20},{12,24},{16,28},{1,13},{5,17},{9,21},{13,25},... | collective-permute-start | bytes 1572872 | tf_op jit(solution)/shard_map/ppermute | solution.py:15
  67.1 30.4 %collective-permute-done = bf16[256,8,128]{2,0,1:T(8,128)(2,1)} collective-permute-done((bf16[256,8,128]{2,0,1:T(8,128)(2,1)}, bf16[256,8,128]{2,0,1:T(8,128)(2,1)}, u32[]{:S(2)}, u32[]{:S(2)}) %collective-permute-start) | collective-permute-done | bytes 524320 | tf_op jit(solution)/shard_map/ppermute | solution.py:15
  101.4 16.8 %collective-permute-start.9 = (bf16[256,8,128]{2,0,1:T(8,128)(2,1)}, bf16[256,8,128]{2,0,1:T(8,128)(2,1)}, u32[]{:S(2)}, u32[]{:S(2)}) collective-permute-start(bf16[256,8,128]{2,0,1:T(8,128)(2,1)} %bitcast.703), channel_id=1, source_target_pairs={{0,12},{4,16},{8,20},{12,24},{16,28},{1,13},{5,17},{9,21},{13,25},... | collective-permute-start | bytes 1572872 | tf_op jit(solution)/shard_map/ppermute | solution.py:15
  127.5 3.5 fusion.320
  131.0 3.4 fusion.323
  134.4 3.4 fusion.326
  174.5 3.6 fusion.79
  197.1 3.6 fusion.129
  231.8 3.6 fusion.78
  235.3 3.5 fusion.77
  238.9 3.5 fusion.76
  242.4 3.6 fusion.75
  245.9 3.6 fusion.74
  249.5 3.5 fusion.73
  253.0 3.5 fusion.72
  256.5 4.5 fusion.318
  268.7 9.8 %collective-permute-done.12 = f32[256,8,128]{2,0,1:T(8,128)} collective-permute-done((f32[256,8,128]{2,0,1:T(8,128)}, f32[256,8,128]{2,0,1:T(8,128)}, u32[]{:S(2)}, u32[]{:S(2)}) %collective-permute-start.12) | collective-permute-done | bytes 1048608 | tf_op jit(solution)/shard_map/ppermute | solution.py:15
  279.8 5.8 %collective-permute-done.15 = f32[256,8,128]{2,0,1:T(8,128)} collective-permute-done((f32[256,8,128]{2,0,1:T(8,128)}, f32[256,8,128]{2,0,1:T(8,128)}, u32[]{:S(2)}, u32[]{:S(2)}) %collective-permute-start.15) | collective-permute-done | bytes 1048608 | tf_op jit(solution)/shard_map/ppermute | solution.py:15
  286.9 12.6 %collective-permute-done.14 = f32[256,8,128]{2,0,1:T(8,128)} collective-permute-done((f32[256,8,128]{2,0,1:T(8,128)}, f32[256,8,128]{2,0,1:T(8,128)}, u32[]{:S(2)}, u32[]{:S(2)}) %collective-permute-start.14) | collective-permute-done | bytes 1048608 | tf_op jit(solution)/shard_map/ppermute | solution.py:15
  299.4 50.5 %collective-permute-start.17 = (f32[256,8,128]{2,0,1:T(8,128)}, f32[256,8,128]{2,0,1:T(8,128)}, u32[]{:S(2)}, u32[]{:S(2)}) collective-permute-start(f32[256,8,128]{2,0,1:T(8,128)} %get-tuple-element.9), channel_id=1, source_target_pairs={{8,0},{12,4},{16,8},{20,12},{24,16},{28,20},{9,1},{13,5},{17,9},{2... | collective-permute-start | bytes 3145736 | tf_op jit(solution)/shard_map/ppermute | solution.py:15
  354.7 80.2 %collective-permute-done.13 = f32[256,8,128]{2,0,1:T(8,128)} collective-permute-done((f32[256,8,128]{2,0,1:T(8,128)}, f32[256,8,128]{2,0,1:T(8,128)}, u32[]{:S(2)}, u32[]{:S(2)}) %collective-permute-start.13) | collective-permute-done | bytes 1048608 | tf_op jit(solution)/shard_map/ppermute | solution.py:15
  438.8 84.5 %collective-permute-done.17 = f32[256,8,128]{2,0,1:T(8,128)} collective-permute-done((f32[256,8,128]{2,0,1:T(8,128)}, f32[256,8,128]{2,0,1:T(8,128)}, u32[]{:S(2)}, u32[]{:S(2)}) %collective-permute-start.17) | collective-permute-done | bytes 1048608 | tf_op jit(solution)/shard_map/ppermute | solution.py:15
  (151 shorter events, 149.1 us)
Async XLA Ops:
  0.6 45.8 %copy-start.13 = (bf16[1,256,8,128]{3,2,1,0:T(8,128)(2,1)S(1)}, bf16[1,256,8,128]{3,2,1,0:T(8,128)(2,1)}, u32[]{:S(2)}) copy-start(bf16[1,256,8,128]{3,2,1,0:T(8,128)(2,1)} %param.8) | copy-start | bytes 1572868
  1.4 62.4 %collective-permute-start.7 = (bf16[256]{0:T(256)(128)(2,1)S(1)}, bf16[256]{0:T(256)(128)(2,1)S(1)}, u32[]{:S(2)}, u32[]{:S(2)}) collective-permute-start(bf16[256]{0:T(256)(128)(2,1)S(1)} %convert_reduce_fusion.1), channel_id=1, source_target_pairs={{0,4},{4,8},{8,12},{12,16},{16,20},{20,24},{24,28},{1,5},{5,9},{9,... | collective-permute-start | bytes 1544 | tf_op jit(solution)/shard_map/ppermute | solution.py:15
  4.8 56.7 %collective-permute-start.6 = (bf16[256]{0:T(256)(128)(2,1)S(1)}, bf16[256]{0:T(256)(128)(2,1)S(1)}, u32[]{:S(2)}, u32[]{:S(2)}) collective-permute-start(bf16[256]{0:T(256)(128)(2,1)S(1)} %convert_reduce_fusion.1), channel_id=1, source_target_pairs={{0,8},{4,12},{8,16},{12,20},{16,24},{20,28},{1,9},{5,13},{9,17},{1... | collective-permute-start | bytes 1544 | tf_op jit(solution)/shard_map/ppermute | solution.py:15
  8.3 43.7 %collective-permute-start.5 = (bf16[256]{0:T(256)(128)(2,1)S(1)}, bf16[256]{0:T(256)(128)(2,1)S(1)}, u32[]{:S(2)}, u32[]{:S(2)}) collective-permute-start(bf16[256]{0:T(256)(128)(2,1)S(1)} %convert_reduce_fusion.1), channel_id=1, source_target_pairs={{0,12},{4,16},{8,20},{12,24},{16,28},{1,13},{5,17},{9,21},{13,25},... | collective-permute-start | bytes 1544 | tf_op jit(solution)/shard_map/ppermute | solution.py:15
  11.2 38.4 %collective-permute-start.4 = (bf16[256]{0:T(256)(128)(2,1)S(1)}, bf16[256]{0:T(256)(128)(2,1)S(1)}, u32[]{:S(2)}, u32[]{:S(2)}) collective-permute-start(bf16[256]{0:T(256)(128)(2,1)S(1)} %convert_reduce_fusion.1), channel_id=1, source_target_pairs={{0,16},{4,20},{8,24},{12,28},{1,17},{5,21},{9,25},{13,29},{2,18},{... | collective-permute-start | bytes 1544 | tf_op jit(solution)/shard_map/ppermute | solution.py:15
  14.4 110.3 %collective-permute-start.3 = (bf16[256,8,128]{2,0,1:T(8,128)(2,1)}, bf16[256,8,128]{2,0,1:T(8,128)(2,1)}, u32[]{:S(2)}, u32[]{:S(2)}) collective-permute-start(bf16[256,8,128]{2,0,1:T(8,128)(2,1)} %bitcast.666), channel_id=1, source_target_pairs={{0,4},{4,8},{8,12},{12,16},{16,20},{20,24},{24,28},{1,5},{5,9},{9,... | collective-permute-start | bytes 1572872 | tf_op jit(solution)/shard_map/ppermute | solution.py:15
  21.3 189.8 %copy-start.14 = (bf16[256,16,128]{2,0,1:T(8,128)(2,1)}, bf16[256,16,128]{2,0,1:T(8,128)(2,1)S(1)}, u32[]{:S(2)}) copy-start(bf16[256,16,128]{2,0,1:T(8,128)(2,1)S(1)} %bitcast_multiply_fusion) | copy-start | bytes 3145732
  48.8 77.8 %copy-start.12 = (bf16[1,256,8,128]{3,2,1,0:T(8,128)(2,1)S(1)}, bf16[1,256,8,128]{3,2,1,0:T(8,128)(2,1)}, u32[]{:S(2)}) copy-start(bf16[1,256,8,128]{3,2,1,0:T(8,128)(2,1)} %param.7) | copy-start | bytes 1572868
  49.6 70.6 %collective-permute-start.2 = (bf16[256,8,128]{2,0,1:T(8,128)(2,1)}, bf16[256,8,128]{2,0,1:T(8,128)(2,1)}, u32[]{:S(2)}, u32[]{:S(2)}) collective-permute-start(bf16[256,8,128]{2,0,1:T(8,128)(2,1)} %bitcast.666), channel_id=1, source_target_pairs={{0,8},{4,12},{8,16},{12,20},{16,24},{20,28},{1,9},{5,13},{9,17},{1... | collective-permute-start | bytes 1572872 | tf_op jit(solution)/shard_map/ppermute | solution.py:15
  52.0 49.4 %collective-permute-start.1 = (bf16[256,8,128]{2,0,1:T(8,128)(2,1)}, bf16[256,8,128]{2,0,1:T(8,128)(2,1)}, u32[]{:S(2)}, u32[]{:S(2)}) collective-permute-start(bf16[256,8,128]{2,0,1:T(8,128)(2,1)} %bitcast.666), channel_id=1, source_target_pairs={{0,12},{4,16},{8,20},{12,24},{16,28},{1,13},{5,17},{9,21},{13,25},... | collective-permute-start | bytes 1572872 | tf_op jit(solution)/shard_map/ppermute | solution.py:15
  61.5 36.0 %collective-permute-start = (bf16[256,8,128]{2,0,1:T(8,128)(2,1)}, bf16[256,8,128]{2,0,1:T(8,128)(2,1)}, u32[]{:S(2)}, u32[]{:S(2)}) collective-permute-start(bf16[256,8,128]{2,0,1:T(8,128)(2,1)} %bitcast.666), channel_id=1, source_target_pairs={{0,16},{4,20},{8,24},{12,28},{1,17},{5,21},{9,25},{13,29},{2,18},{... | collective-permute-start | bytes 1572872 | tf_op jit(solution)/shard_map/ppermute | solution.py:15
  63.8 99.0 %collective-permute-start.11 = (bf16[256,8,128]{2,0,1:T(8,128)(2,1)}, bf16[256,8,128]{2,0,1:T(8,128)(2,1)}, u32[]{:S(2)}, u32[]{:S(2)}) collective-permute-start(bf16[256,8,128]{2,0,1:T(8,128)(2,1)} %bitcast.701), channel_id=1, source_target_pairs={{0,4},{4,8},{8,12},{12,16},{16,20},{20,24},{24,28},{1,5},{5,9},{9,... | collective-permute-start | bytes 1572872 | tf_op jit(solution)/shard_map/ppermute | solution.py:15
  97.5 59.9 %collective-permute-start.10 = (bf16[256,8,128]{2,0,1:T(8,128)(2,1)}, bf16[256,8,128]{2,0,1:T(8,128)(2,1)}, u32[]{:S(2)}, u32[]{:S(2)}) collective-permute-start(bf16[256,8,128]{2,0,1:T(8,128)(2,1)} %bitcast.702), channel_id=1, source_target_pairs={{0,8},{4,12},{8,16},{12,20},{16,24},{20,28},{1,9},{5,13},{9,17},{1... | collective-permute-start | bytes 1572872 | tf_op jit(solution)/shard_map/ppermute | solution.py:15
  101.4 54.1 %collective-permute-start.9 = (bf16[256,8,128]{2,0,1:T(8,128)(2,1)}, bf16[256,8,128]{2,0,1:T(8,128)(2,1)}, u32[]{:S(2)}, u32[]{:S(2)}) collective-permute-start(bf16[256,8,128]{2,0,1:T(8,128)(2,1)} %bitcast.703), channel_id=1, source_target_pairs={{0,12},{4,16},{8,20},{12,24},{16,28},{1,13},{5,17},{9,21},{13,25},... | collective-permute-start | bytes 1572872 | tf_op jit(solution)/shard_map/ppermute | solution.py:15
  120.2 30.1 %collective-permute-start.8 = (bf16[256,8,128]{2,0,1:T(8,128)(2,1)}, bf16[256,8,128]{2,0,1:T(8,128)(2,1)}, u32[]{:S(2)}, u32[]{:S(2)}) collective-permute-start(bf16[256,8,128]{2,0,1:T(8,128)(2,1)} %bitcast.704), channel_id=1, source_target_pairs={{0,16},{4,20},{8,24},{12,28},{1,17},{5,21},{9,25},{13,29},{2,18},{... | collective-permute-start | bytes 1572872 | tf_op jit(solution)/shard_map/ppermute | solution.py:15
  224.9 53.6 %collective-permute-start.12 = (f32[256,8,128]{2,0,1:T(8,128)}, f32[256,8,128]{2,0,1:T(8,128)}, u32[]{:S(2)}, u32[]{:S(2)}) collective-permute-start(f32[256,8,128]{2,0,1:T(8,128)} %get-tuple-element.10), channel_id=1, source_target_pairs={{4,0},{8,4},{12,8},{16,12},{20,16},{24,20},{28,24},{5,1},{9,5},{13... | collective-permute-start | bytes 3145736 | tf_op jit(solution)/shard_map/ppermute | solution.py:15
  226.9 58.7 %collective-permute-start.15 = (f32[256,8,128]{2,0,1:T(8,128)}, f32[256,8,128]{2,0,1:T(8,128)}, u32[]{:S(2)}, u32[]{:S(2)}) collective-permute-start(f32[256,8,128]{2,0,1:T(8,128)} %get-tuple-element.11), channel_id=1, source_target_pairs={{16,0},{20,4},{24,8},{28,12},{17,1},{21,5},{25,9},{29,13},{18,2},{... | collective-permute-start | bytes 3145736 | tf_op jit(solution)/shard_map/ppermute | solution.py:15
  228.2 71.3 %collective-permute-start.14 = (f32[256,8,128]{2,0,1:T(8,128)}, f32[256,8,128]{2,0,1:T(8,128)}, u32[]{:S(2)}, u32[]{:S(2)}) collective-permute-start(f32[256,8,128]{2,0,1:T(8,128)} %get-tuple-element.12), channel_id=1, source_target_pairs={{12,0},{16,4},{20,8},{24,12},{28,16},{13,1},{17,5},{21,9},{25,13},... | collective-permute-start | bytes 3145736 | tf_op jit(solution)/shard_map/ppermute | solution.py:15
  229.5 205.4 %collective-permute-start.13 = (f32[256,8,128]{2,0,1:T(8,128)}, f32[256,8,128]{2,0,1:T(8,128)}, u32[]{:S(2)}, u32[]{:S(2)}) collective-permute-start(f32[256,8,128]{2,0,1:T(8,128)} %get-tuple-element.13), channel_id=1, source_target_pairs={{8,0},{12,4},{16,8},{20,12},{24,16},{28,20},{9,1},{13,5},{17,9},{2... | collective-permute-start | bytes 3145736 | tf_op jit(solution)/shard_map/ppermute | solution.py:15
  261.0 177.8 %collective-permute-start.16 = (f32[256,8,128]{2,0,1:T(8,128)}, f32[256,8,128]{2,0,1:T(8,128)S(1)}, u32[]{:S(2)}, u32[]{:S(2)}) collective-permute-start(f32[256,8,128]{2,0,1:T(8,128)} %get-tuple-element.6), channel_id=1, source_target_pairs={{4,0},{8,4},{12,8},{16,12},{20,16},{24,20},{28,24},{5,1},{9,5},{13... | collective-permute-start | bytes 3145736 | tf_op jit(solution)/shard_map/ppermute | solution.py:15
  265.9 85.4 %copy-start.2 = (bf16[2,256,1280]{1,2,0:T(8,128)(2,1)S(1)}, bf16[2,256,1280]{1,2,0:T(8,128)(2,1)}, u32[]{:S(2)}) copy-start(bf16[2,256,1280]{1,2,0:T(8,128)(2,1)} %copy-done.1) | copy-start | bytes 3932164
  278.5 160.3 %collective-permute-start.19 = (f32[256,8,128]{2,0,1:T(8,128)}, f32[256,8,128]{2,0,1:T(8,128)}, u32[]{:S(2)}, u32[]{:S(2)}) collective-permute-start(f32[256,8,128]{2,0,1:T(8,128)} %get-tuple-element.7), channel_id=1, source_target_pairs={{16,0},{20,4},{24,8},{28,12},{17,1},{21,5},{25,9},{29,13},{18,2},{... | collective-permute-start | bytes 3145736 | tf_op jit(solution)/shard_map/ppermute | solution.py:15
  285.6 153.3 %collective-permute-start.18 = (f32[256,8,128]{2,0,1:T(8,128)}, f32[256,8,128]{2,0,1:T(8,128)}, u32[]{:S(2)}, u32[]{:S(2)}) collective-permute-start(f32[256,8,128]{2,0,1:T(8,128)} %get-tuple-element.8), channel_id=1, source_target_pairs={{12,0},{16,4},{20,8},{24,12},{28,16},{13,1},{17,5},{21,9},{25,13},... | collective-permute-start | bytes 3145736 | tf_op jit(solution)/shard_map/ppermute | solution.py:15
  299.4 223.8 %collective-permute-start.17 = (f32[256,8,128]{2,0,1:T(8,128)}, f32[256,8,128]{2,0,1:T(8,128)}, u32[]{:S(2)}, u32[]{:S(2)}) collective-permute-start(f32[256,8,128]{2,0,1:T(8,128)} %get-tuple-element.9), channel_id=1, source_target_pairs={{8,0},{12,4},{16,8},{20,12},{24,16},{28,20},{9,1},{13,5},{17,9},{2... | collective-permute-start | bytes 3145736 | tf_op jit(solution)/shard_map/ppermute | solution.py:15
  (22 other events, 116.8 us)
where the time goes:
time: 533 us; the launch traced here: 527 us
  waiting for transfers between devices  226 us (42%)
  starting transfers between devices  113 us (21%)
  matrix products  109 us (20%)
  local copies, waits for them, and re-layouts  41.3 us (8%)
  blocking collectives  25 us (5%)
  other arithmetic  10.9 us (2%)
    ppermute x20, waiting for transfers between devices, from_behind(): return lax.ppermute(shard, axis, pairs)  226 us
    ppermute x20, starting transfers between devices, from_behind(): return lax.ppermute(shard, axis, pairs)  113 us
    unnamed x70, local copies, waits for them, and re-layouts  32.9 us
    dot_general x8, matrix products, on_device(): jnp.einsum('gtj,tgd->jd', prob_b16, grad_group, preferred_element_type=jn...  28.3 us
    sub x8, matrix products, on_device(): raised = jnp.exp(logits - top_score[:, :, None])  27.1 us
    dot_general x8, matrix products, on_device(): jnp.einsum('gtj,jd->tgd', prob_b16, value_block, preferred_element_type=j...  25.7 us
    psum x1, blocking collectives, on_device(): count_all = lax.psum(jnp.sum(loss_mask).astype(jnp.float32), ('ctx', 'dp'))  25 us
    dot_general x8, matrix products, on_device(): jnp.einsum('gtj,jd->tgd', grad_logits, key_block, preferred_element_type=...  12.6 us
  transfers between devices with their start and end apart: 20, of which 7 were waited for; matrix products, arithmetic and copies ran while one was open for 18% of the time, Pallas kernels for 0%

commit v1 on v0

v1 whole, which is shorter than its diff:
```python
import functools
import math

import jax
import jax.numpy as jnp
from jax import lax
from jax.experimental import pallas as pl
from jax.experimental.pallas import tpu as pltpu
from jax.sharding import PartitionSpec as P

WINDOW = 1024
SCALE = 168.0 ** (-0.5)
STRIP = 128
MASKED = -1e30


def head_grads(head, rows, q_ref, g_ref, ext, bias, acc, dq_ref):
    span = WINDOW + STRIP
    for strip in range(rows // STRIP):
        low = strip * STRIP
        query = q_ref[head, strip]
        grad = g_ref[head, strip]
        key = ext[head, 0, low : low + span, :]
        value = ext[head, 1, low : low + span, :]
        logits = lax.dot_general(
            key, query, (((1,), (1,)), ((), ())), preferred_element_type=jnp.float32
        )
        logits = logits * (SCALE * math.log2(math.e)) + bias[strip]
        top = jnp.max(logits, axis=0, keepdims=True)
        raised = jnp.exp2(logits - top)
        prob = raised * (1.0 / jnp.sum(raised, axis=0, keepdims=True))
        grad_prob = lax.dot_general(
            value, grad, (((1,), (1,)), ((), ())), preferred_element_type=jnp.float32
        )
        delta = jnp.sum(prob * grad_prob, axis=0, keepdims=True)
        grad_logit = (prob * (grad_prob - delta)).astype(jnp.bfloat16)
        dq_ref[head, strip] = lax.dot_general(
            grad_logit, key, (((0,), (0,)), ((), ())), preferred_element_type=jnp.float32
        )
        parts = (
            jnp.dot(grad_logit, query, preferred_element_type=jnp.float32),
            jnp.dot(prob.astype(jnp.bfloat16), grad, preferred_element_type=jnp.float32),
        )
        for kind, part in enumerate(parts):
            if strip == 0:
                acc[kind, :span] = part
            else:
                cut = span - STRIP
                acc[kind, low : low + cut] += part[:cut]
                acc[kind, low + cut : low + span] = part[cut:]


def fill_bias(rows, mark_ref, low_ref, marks, bias):
    hops = WINDOW // rows
    first = mark_ref[0:1, 0:1]
    before = jnp.zeros((1, 1), jnp.float32)
    for hop in range(hops):
        earlier = jnp.where(marks[hop, 0:1, :] < first, 1.0, 0.0)
        before += jnp.sum(earlier, axis=1, keepdims=True)
    for strip in range(rows // STRIP):
        own = low_ref[strip, 0:1, :].astype(jnp.float32)
        start = jnp.where(own > 0.0, own + WINDOW, before) - strip * STRIP
        shape = bias.shape[1:]
        row = lax.broadcasted_iota(jnp.int32, (1, shape[1]), 1) & (STRIP - 1)
        lowest = jnp.maximum(start.astype(jnp.int32), row + 1)
        col = lax.broadcasted_iota(jnp.int32, shape, 0)
        ok = (col >= lowest) & (col <= row + WINDOW)
        bias[strip] = jnp.where(ok, 0.0, MASKED)


def kernel(
    n, rows, q_ref, g_ref, kv_ref, mark_ref, low_ref, dq_ref, dkv_ref,
    ext, sent, back, marks, bias, acc,
    mark_send, mark_recv, kv_send, kv_recv, back_send, back_recv,
):
    hops = WINDOW // rows
    heads = kv_ref.shape[0]
    me = lax.axis_index("ctx")

    def mark_copy(d):
        return pltpu.make_async_remote_copy(
            src_ref=mark_ref, dst_ref=marks.at[d - 1],
            send_sem=mark_send.at[d - 1], recv_sem=mark_recv.at[d - 1],
            device_id={"ctx": me + d}, device_id_type=pl.DeviceIdType.MESH,
        )

    def kv_copy(head, d):
        return pltpu.make_async_remote_copy(
            src_ref=kv_ref.at[head],
            dst_ref=ext.at[head, :, pl.ds(WINDOW - d * rows, rows), :],
            send_sem=kv_send.at[head, d - 1], recv_sem=kv_recv.at[head, d - 1],
            device_id={"ctx": me + d}, device_id_type=pl.DeviceIdType.MESH,
        )

    def back_copy(head, d):
        return pltpu.make_async_remote_copy(
            src_ref=sent.at[head, d - 1], dst_ref=back.at[head, d - 1],
            send_sem=back_send.at[head, d - 1], recv_sem=back_recv.at[head, d - 1],
            device_id={"ctx": me - d}, device_id_type=pl.DeviceIdType.MESH,
        )

    barrier = pltpu.get_barrier_semaphore()
    for d in range(1, hops + 1):
        @pl.when(me + d < n)
        def _():
            pl.semaphore_signal(barrier, inc=1, device_id={"ctx": me + d},
                                device_id_type=pl.DeviceIdType.MESH)

        @pl.when(me >= d)
        def _():
            pl.semaphore_signal(barrier, inc=1, device_id={"ctx": me - d},
                                device_id_type=pl.DeviceIdType.MESH)
    pl.semaphore_wait(barrier, jnp.minimum(me, hops) + jnp.minimum(n - 1 - me, hops))

    for d in range(1, hops + 1):
        @pl.when(me + d < n)
        def _():
            mark_copy(d).start()

    def send_head(head, carry):
        for d in range(1, hops + 1):
            @pl.when(me + d < n)
            def _():
                kv_copy(head, d).start()
        ext[head, :, WINDOW : WINDOW + rows, :] = kv_ref[head]
        for d in range(1, hops + 1):
            @pl.when(me < d)
            def _():
                ext[head, :, WINDOW - d * rows : WINDOW - (d - 1) * rows, :] = jnp.zeros(
                    (2, rows, kv_ref.shape[3]), kv_ref.dtype
                )
        return carry

    lax.fori_loop(0, heads, send_head, 0)

    for d in range(1, hops + 1):
        @pl.when(me < d)
        def _():
            marks[d - 1] = jnp.full(mark_ref.shape, -1, jnp.int32)

        @pl.when(me >= d)
        def _():
            mark_copy(d).wait_recv()
    fill_bias(rows, mark_ref, low_ref, marks, bias)

    def do_head(head, carry):
        for d in range(1, hops + 1):
            @pl.when(me >= d)
            def _():
                kv_copy(head, d).wait_recv()
        head_grads(head, rows, q_ref, g_ref, ext, bias, acc, dq_ref)
        for d in range(1, hops + 1):
            low = WINDOW - d * rows
            sent[head, d - 1] = acc[:, low : low + rows, :].astype(sent.dtype)

            @pl.when(me >= d)
            def _():
                back_copy(head, d).start()
        dkv_ref[head] = acc[:, WINDOW : WINDOW + rows, :]
        return carry

    lax.fori_loop(0, heads, do_head, 0)

    def finish_head(head, carry):
        for d in range(1, hops + 1):
            @pl.when(me + d < n)
            def _():
                back_copy(head, d).wait_recv()
                dkv_ref[head] += back[head, d - 1].astype(jnp.float32)
        for d in range(1, hops + 1):
            @pl.when(me + d < n)
            def _():
                kv_copy(head, d).wait_send()

            @pl.when(me >= d)
            def _():
                back_copy(head, d).wait_send()
        return carry

    lax.fori_loop(0, heads, finish_head, 0)
    for d in range(1, hops + 1):
        @pl.when(me + d < n)
        def _():
            mark_copy(d).wait_send()


def on_device(queries, keys, values, d_out, loss_mask, turn_ids):
    rows, heads_q, depth = queries.shape[1:]
    heads = keys.shape[2]
    group = heads_q // heads
    n = lax.axis_size("ctx")
    hops = WINDOW // rows
    strips = rows // STRIP
    wide = group * STRIP
    count_all = lax.psum(jnp.sum(loss_mask).astype(jnp.float32), ("ctx", "dp"))
    factor = rows * n * lax.axis_size("dp") / count_all

    def by_strip(array):
        array = array.reshape(strips, STRIP, heads, group, depth)
        return array.transpose(2, 0, 3, 1, 4).reshape(heads, strips, wide, depth)

    q = by_strip(queries[0])
    g = by_strip(d_out[0] * loss_mask[0][:, None, None].astype(jnp.bfloat16))
    kv = jnp.stack([keys[0], values[0]]).transpose(2, 0, 1, 3)
    turn = turn_ids[0]
    own_low = jnp.sum((turn[None, :] < turn[:, None]).astype(jnp.int32), axis=1)
    own_low = own_low.reshape(strips, 1, 1, STRIP)
    own_low = jnp.broadcast_to(own_low, (strips, 8, group, STRIP)).reshape(strips, 8, wide)
    mark = jnp.broadcast_to(turn[None, :], (8, rows))
    vmem = pl.BlockSpec(memory_space=pltpu.VMEM)
    span = WINDOW + rows
    dq, dkv = pl.pallas_call(
        functools.partial(kernel, n, rows),
        out_shape=(
            jax.ShapeDtypeStruct((heads, strips, wide, depth), jnp.float32),
            jax.ShapeDtypeStruct((heads, 2, rows, depth), jnp.float32),
        ),
        in_specs=[vmem] * 5,
        out_specs=(vmem, vmem),
        scratch_shapes=[
            pltpu.VMEM((heads, 2, span, depth), jnp.bfloat16),
            pltpu.VMEM((heads, hops, 2, rows, depth), jnp.bfloat16),
            pltpu.VMEM((heads, hops, 2, rows, depth), jnp.bfloat16),
            pltpu.VMEM((hops, 8, rows), jnp.int32),
            pltpu.VMEM((strips, WINDOW + STRIP, wide), jnp.float32),
            pltpu.VMEM((2, span, depth), jnp.float32),
            pltpu.SemaphoreType.DMA((hops,)),
            pltpu.SemaphoreType.DMA((hops,)),
            pltpu.SemaphoreType.DMA((heads, hops)),
            pltpu.SemaphoreType.DMA((heads, hops)),
            pltpu.SemaphoreType.DMA((heads, hops)),
            pltpu.SemaphoreType.DMA((heads, hops)),
        ],
        compiler_params=pltpu.CompilerParams(
            collective_id=0, has_side_effects=True, vmem_limit_bytes=56 << 20
        ),
    )(q, g, kv, mark, own_low)
    d_q = (dq * (factor * SCALE)).astype(jnp.bfloat16)
    d_q = d_q.reshape(heads, strips, group, STRIP, depth).transpose(1, 3, 0, 2, 4)
    d_queries = d_q.reshape(1, rows, heads_q, depth)
    d_keys = (dkv[:, 0] * (factor * SCALE)).astype(jnp.bfloat16).transpose(1, 0, 2)[None]
    d_values = (dkv[:, 1] * factor).astype(jnp.bfloat16).transpose(1, 0, 2)[None]
    return (d_queries, d_keys, d_values)


def solution(mesh):
    spec = P("dp", "ctx", "head", None)
    return jax.shard_map(
        on_device,
        mesh=mesh,
        in_specs=(spec, spec, spec, spec, P("dp", "ctx"), P("dp", "ctx")),
        out_specs=(spec, spec, spec),
        check_vma=False,
    )
```

time: 533 us -> 227 us (0.43)
  the two profiles are of different devices: /device:TPU:8 before, /device:TPU:0 now
where the time goes in v1:
time: 227 us
  Pallas kernels  179 us (79%)
  blocking collectives  30 us (13%)
  local copies, waits for them, and re-layouts  9.8 us (4%)
  other arithmetic  6.09 us (3%)
    pallas_call x1, Pallas kernels, on_device(): pl.pallas_call(functools.partial(kernel, n, rows), out_shape=(jax.ShapeDt...  179 us
    psum x1, blocking collectives, on_device(): count_all = lax.psum(jnp.sum(loss_mask).astype(jnp.float32), ('ctx', 'dp'))  30 us
    unnamed x14, local copies, waits for them, and re-layouts  4.61 us

profile of v1, /device:TPU:0, one launch (start us, length us, event | category | flops | bytes accessed | tf_op | source)
XLA Modules:
  0.0 226.7 jit_solution(4610892429124093303)
XLA Ops:
  0.6 0.9 convert_reduce_fusion
  1.6 0.6 broadcast_in_dim.29.low_ref
  2.2 1.3 broadcast_in_dim.25.mark_ref
  3.5 0.0 copy-start.3
  3.5 0.0 copy-start.1
  3.5 1.2 copy.18
  4.7 1.1 copy.19
  5.8 0.0 copy-start.2
  5.8 1.1 maximum_bitcast_fusion.kv_ref
  6.9 0.0 copy-done.3
  6.9 0.0 copy-done.1
  6.9 1.2 copy_multiply_fusion
  8.2 0.0 copy-done.2
  8.2 1.3 copy.16
  9.4 178.7 %shard_map.85 = (f32[8,2,256,128]{3,2,1,0:T(8,128)}, f32[8,2,256,128]{3,2,1,0:T(8,128)}) custom-call(bf16[8,2,256,128]{3,2,1,0:T(8,128)(2,1)} %bitcast.35, bf16[8,2,256,128]{3,2,1,0:T(8,128)(2,1)} %bitcast.34, bf16[8,2,256,128]{3,2,1,0:T(8,128)(2,1)} %maximum_bitcast_fusion.kv_ref, s32[8,256]{1,0:T(8,128)} %broadcast_in_dim.25.mark_ref, ...), custom_call_target="tpu_custom_call" | custom-call | tf_op jit(solution)/shard_map/pallas_call | solution.py:212
  188.1 0.6 reduce_sum.19
  189.4 30.0 %psum.7 = f32[]{:T(128)} all-reduce(f32[]{:T(128)S(6)} %convert_element_type.35), channel_id=1, replica_groups=mesh['ctx'=8,'head'=2,'dp'=2] {'ctx','dp'}, use_global_device_ids=true, to_apply=%region_2.0 | all-reduce | flops 1 | bytes 8 | tf_op jit(solution)/shard_map/psum | solution.py:195
  220.1 0.0 copy-start
  220.1 1.9 fusion.1
  222.1 1.1 copy.21
  223.2 1.1 copy.22
  224.3 0.0 copy-done
  224.4 0.2 multiply_convert_fusion
  224.6 2.0 copy.20
  (3 shorter events, 0.0 us)
Async XLA Ops:
  3.5 3.4 %copy-start.3 = (s32[1,256]{1,0:T(1,128)S(1)}, s32[1,256]{1,0:T(1,128)}, u32[]{:S(2)}) copy-start(s32[1,256]{1,0:T(1,128)} %param.10) | copy-start | bytes 3076
  3.5 3.5 %copy-start.1 = (bf16[1,256,16,128]{3,2,1,0:T(8,128)(2,1)S(1)}, bf16[1,256,16,128]{3,2,1,0:T(8,128)(2,1)}, u32[]{:S(2)}) copy-start(bf16[1,256,16,128]{3,2,1,0:T(8,128)(2,1)} %param.9) | copy-start | bytes 3145732
  5.8 2.4 %copy-start.2 = (bf16[1,256,16,128]{3,2,1,0:T(8,128)(2,1)S(1)}, bf16[1,256,16,128]{3,2,1,0:T(8,128)(2,1)}, u32[]{:S(2)}) copy-start(bf16[1,256,16,128]{3,2,1,0:T(8,128)(2,1)} %param.6) | copy-start | bytes 3145732
  220.1 4.2 %copy-start = (f32[8,2,256,128]{3,2,1,0:T(8,128)S(1)}, f32[8,2,256,128]{3,2,1,0:T(8,128)}, u32[]{:S(2)}) copy-start(f32[8,2,256,128]{3,2,1,0:T(8,128)} %get-tuple-element.5) | copy-start | bytes 6291460

commit v2 on v1

--- a/solution.py
+++ b/solution.py
@@ -12,6 +12,7 @@
 SCALE = 168.0 ** (-0.5)
 STRIP = 128
 MASKED = -1e30
+AHEAD = 2
 
 
 def head_grads(head, rows, q_ref, g_ref, ext, bias, acc, dq_ref):
@@ -69,59 +70,101 @@
 
 
 def kernel(
-    n, rows, q_ref, g_ref, kv_ref, mark_ref, low_ref, dq_ref, dkv_ref,
-    ext, sent, back, marks, bias, acc,
-    mark_send, mark_recv, kv_send, kv_recv, back_send, back_recv,
+    n, pairs, rows, q_ref, g_ref, kv_ref, mark_ref, low_ref, count_ref,
+    dq_ref, dkv_ref, total_ref,
+    ext, sent, back, marks, bias, acc, count, count_in,
+    mark_send, mark_recv, kv_send, kv_recv, back_send, back_recv, count_send, count_recv,
 ):
     hops = WINDOW // rows
     heads = kv_ref.shape[0]
     me = lax.axis_index("ctx")
+    odd = me % 2
+    other = me + 1 - 2 * odd
+    bits = [("ctx", 1 << b) for b in range(n.bit_length() - 1)]
+    bits += [("dp", 1 << b) for b in range(pairs.bit_length() - 1)]
+
+    def remote(src, dst, send, recv, device):
+        return pltpu.make_async_remote_copy(
+            src_ref=src, dst_ref=dst, send_sem=send, recv_sem=recv,
+            device_id=device, device_id_type=pl.DeviceIdType.MESH,
+        )
+
+    def partner(axis, bit):
+        at = lax.axis_index(axis)
+        return {axis: at + bit - 2 * bit * ((at // bit) % 2)}
 
     def mark_copy(d):
-        return pltpu.make_async_remote_copy(
-            src_ref=mark_ref, dst_ref=marks.at[d - 1],
-            send_sem=mark_send.at[d - 1], recv_sem=mark_recv.at[d - 1],
-            device_id={"ctx": me + d}, device_id_type=pl.DeviceIdType.MESH,
-        )
+        return remote(mark_ref, marks.at[d - 1], mark_send.at[d - 1], mark_recv.at[d - 1],
+                      {"ctx": me + d})
+
+    def count_copy(k):
+        return remote(count.at[k], count_in.at[k], count_send.at[k], count_recv.at[k],
+                      partner(*bits[k]))
+
+    def slot(head, d):
+        return ext.at[head, :, pl.ds(WINDOW - d * rows, rows), :]
 
     def kv_copy(head, d):
-        return pltpu.make_async_remote_copy(
-            src_ref=kv_ref.at[head],
-            dst_ref=ext.at[head, :, pl.ds(WINDOW - d * rows, rows), :],
-            send_sem=kv_send.at[head, d - 1], recv_sem=kv_recv.at[head, d - 1],
-            device_id={"ctx": me + d}, device_id_type=pl.DeviceIdType.MESH,
-        )
+        if d == 1:
+            return remote(slot(head, 2), slot(head, 1), kv_send.at[head, 0],
+                          kv_recv.at[head, 0], {"ctx": other})
+        src = kv_ref.at[head] if d == 2 else slot(head, d - 2)
+        return remote(src, slot(head, d), kv_send.at[head, d - 1], kv_recv.at[head, d - 1],
+                      {"ctx": me + 2})
+
+    def own_across(head):
+        return remote(kv_ref.at[head], slot(head, 1), kv_send.at[head, 0],
+                      kv_recv.at[head, 0], {"ctx": other})
 
     def back_copy(head, d):
-        return pltpu.make_async_remote_copy(
-            src_ref=sent.at[head, d - 1], dst_ref=back.at[head, d - 1],
-            send_sem=back_send.at[head, d - 1], recv_sem=back_recv.at[head, d - 1],
-            device_id={"ctx": me - d}, device_id_type=pl.DeviceIdType.MESH,
-        )
+        return remote(sent.at[head, d - 1], back.at[head, d - 1], back_send.at[head, d - 1],
+                      back_recv.at[head, d - 1], {"ctx": other if d == 1 else me - 2})
+
+    def add_in(head, d, taken):
+        sent[head, d - 1] = (
+            sent[head, d - 1].astype(jnp.float32) + back[head, taken - 1].astype(jnp.float32)
+        ).astype(sent.dtype)
 
     barrier = pltpu.get_barrier_semaphore()
+
+    def greet(device):
+        pl.semaphore_signal(barrier, inc=1, device_id=device,
+                            device_id_type=pl.DeviceIdType.MESH)
+
     for d in range(1, hops + 1):
         @pl.when(me + d < n)
         def _():
-            pl.semaphore_signal(barrier, inc=1, device_id={"ctx": me + d},
-                                device_id_type=pl.DeviceIdType.MESH)
+            greet({"ctx": me + d})
 
         @pl.when(me >= d)
         def _():
-            pl.semaphore_signal(barrier, inc=1, device_id={"ctx": me - d},
-                                device_id_type=pl.DeviceIdType.MESH)
-    pl.semaphore_wait(barrier, jnp.minimum(me, hops) + jnp.minimum(n - 1 - me, hops))
+            greet({"ctx": me - d})
+    far = [b for b in bits if b[0] == "dp" or b[1] > hops]
+    for b in far:
+        greet(partner(*b))
+    pl.semaphore_wait(
+        barrier, jnp.minimum(me, hops) + jnp.minimum(n - 1 - me, hops) + len(far)
+    )
+
+    def send_own(head):
+        @pl.when(me + 2 < n)
+        def _():
+            kv_copy(head, 2).start()
+
+        @pl.when(odd == 0)
+        def _():
+            own_across(head).start()
 
     for d in range(1, hops + 1):
         @pl.when(me + d < n)
         def _():
             mark_copy(d).start()
-
-    def send_head(head, carry):
-        for d in range(1, hops + 1):
-            @pl.when(me + d < n)
-            def _():
-                kv_copy(head, d).start()
+    for head in range(min(AHEAD, heads)):
+        send_own(head)
+    count[0] = count_ref[...]
+    count_copy(0).start()
+
+    def place_own(head, carry):
         ext[head, :, WINDOW : WINDOW + rows, :] = kv_ref[head]
         for d in range(1, hops + 1):
             @pl.when(me < d)
@@ -131,7 +174,7 @@
                 )
         return carry
 
-    lax.fori_loop(0, heads, send_head, 0)
+    lax.fori_loop(0, heads, place_own, 0)
 
     for d in range(1, hops + 1):
         @pl.when(me < d)
@@ -143,45 +186,150 @@
             mark_copy(d).wait_recv()
     fill_bias(rows, mark_ref, low_ref, marks, bias)
 
-    def do_head(head, carry):
+    def step(s, carry):
+        for k in range(len(bits)):
+            @pl.when(s == k)
+            def _():
+                count_copy(k).wait_recv()
+                count[k + 1] = count[k] + count_in[k]
+                if k + 1 < len(bits):
+                    count_copy(k + 1).start()
+
+        @pl.when(s + AHEAD < heads)
+        def _():
+            send_own(s + AHEAD)
+
+        @pl.when(s < heads)
+        def _():
+            @pl.when(me >= 2)
+            def _():
+                kv_copy(s, 2).wait_recv()
+
+                @pl.when(odd == 1)
+                def _():
+                    kv_copy(s, 1).start()
+
+                @pl.when(me + 2 < n)
+                def _():
+                    kv_copy(s, 4).start()
+
+            @pl.when(odd == 1)
+            def _():
+                kv_copy(s, 1).wait_recv()
+
+                @pl.when(me + 2 < n)
+                def _():
+                    kv_copy(s, 3).start()
+
+        @pl.when((s >= 1) & (s < heads + 1) & (odd == 0) & (me >= 2))
+        def _():
+            kv_copy(s - 1, 1).wait_recv()
+
+            @pl.when(me + 2 < n)
+            def _():
+                kv_copy(s - 1, 3).start()
+
+        @pl.when((s >= 3) & (s < heads + 3))
+        def _():
+            head = s - 3
+
+            @pl.when(me >= 1)
+            def _():
+                @pl.when(me + 2 < n)
+                def _():
+                    back_copy(head, 3).wait_recv()
+                    add_in(head, 1, 3)
+
+                back_copy(head, 1).start()
+
+            @pl.when((odd == 0) & (me >= 2))
+            def _():
+                @pl.when(me + 2 < n)
+                def _():
+                    back_copy(head, 4).wait_recv()
+                    add_in(head, 2, 4)
+
+                back_copy(head, 2).start()
+
+        @pl.when((s >= 4) & (s < heads + 4) & (odd == 1) & (me >= 2))
+        def _():
+            head = s - 4
+
+            @pl.when(me + 2 < n)
+            def _():
+                back_copy(head, 4).wait_recv()
+                add_in(head, 2, 4)
+
+            back_copy(head, 1).wait_recv()
+            add_in(head, 2, 1)
+            back_copy(head, 2).start()
+
+        @pl.when(s >= 5)
+        def _():
+            head = s - 5
+
+            @pl.when(odd == 0)
+            def _():
+                back_copy(head, 1).wait_recv()
+                dkv_ref[head] += back[head, 0].astype(jnp.float32)
+
+            @pl.when(me + 2 < n)
+            def _():
+                back_copy(head, 2).wait_recv()
+                dkv_ref[head] += back[head, 1].astype(jnp.float32)
+
+        @pl.when((s >= 2) & (s < heads + 2))
+        def _():
+            head = s - 2
+            for d in (3, 4):
+                @pl.when(me >= d)
+                def _():
+                    kv_copy(head, d).wait_recv()
+            head_grads(head, rows, q_ref, g_ref, ext, bias, acc, dq_ref)
+            for d in (4, 3, 2, 1):
+                low = WINDOW - d * rows
+                sent[head, d - 1] = acc[:, low : low + rows, :].astype(sent.dtype)
+                if d > 2:
+                    @pl.when(me >= d)
+                    def _():
+                        back_copy(head, d).start()
+            dkv_ref[head] = acc[:, WINDOW : WINDOW + rows, :]
+
+        return carry
+
+    lax.fori_loop(0, heads + 5, step, 0)
+
+    def drain(head, carry):
+        @pl.when((odd == 0) | (me >= 2))
+        def _():
+            kv_copy(head, 1).wait_send()
+
+        @pl.when(me + 2 < n)
+        def _():
+            kv_copy(head, 2).wait_send()
+
+            @pl.when(me >= 1)
+            def _():
+                kv_copy(head, 3).wait_send()
+
+            @pl.when(me >= 2)
+            def _():
+                kv_copy(head, 4).wait_send()
+
         for d in range(1, hops + 1):
             @pl.when(me >= d)
             def _():
-                kv_copy(head, d).wait_recv()
-        head_grads(head, rows, q_ref, g_ref, ext, bias, acc, dq_ref)
-        for d in range(1, hops + 1):
-            low = WINDOW - d * rows
-            sent[head, d - 1] = acc[:, low : low + rows, :].astype(sent.dtype)
-
-            @pl.when(me >= d)
-            def _():
-                back_copy(head, d).start()
-        dkv_ref[head] = acc[:, WINDOW : WINDOW + rows, :]
-        return carry
-
-    lax.fori_loop(0, heads, do_head, 0)
-
-    def finish_head(head, carry):
-        for d in range(1, hops + 1):
-            @pl.when(me + d < n)
-            def _():
-                back_copy(head, d).wait_recv()
-                dkv_ref[head] += back[head, d - 1].astype(jnp.float32)
-        for d in range(1, hops + 1):
-            @pl.when(me + d < n)
-            def _():
-                kv_copy(head, d).wait_send()
-
-            @pl.when(me >= d)
-            def _():
                 back_copy(head, d).wait_send()
         return carry
 
-    lax.fori_loop(0, heads, finish_head, 0)
+    lax.fori_loop(0, heads, drain, 0)
     for d in range(1, hops + 1):
         @pl.when(me + d < n)
         def _():
             mark_copy(d).wait_send()
+    for k in range(len(bits)):
+        count_copy(k).wait_send()
+    total_ref[...] = count[len(bits)]
 
 
 def on_device(queries, keys, values, d_out, loss_mask, turn_ids):
@@ -192,8 +340,9 @@
     hops = WINDOW // rows
     strips = rows // STRIP
     wide = group * STRIP
-    count_all = lax.psum(jnp.sum(loss_mask).astype(jnp.float32), ("ctx", "dp"))
-    factor = rows * n * lax.axis_size("dp") / count_all
+    pairs = lax.axis_size("dp")
+    rounds = n.bit_length() + pairs.bit_length() - 2
+    count = jnp.full((8, 128), jnp.sum(loss_mask).astype(jnp.float32))
 
     def by_strip(array):
         array = array.reshape(strips, STRIP, heads, group, depth)
@@ -209,14 +358,15 @@
     mark = jnp.broadcast_to(turn[None, :], (8, rows))
     vmem = pl.BlockSpec(memory_space=pltpu.VMEM)
     span = WINDOW + rows
-    dq, dkv = pl.pallas_call(
-        functools.partial(kernel, n, rows),
+    dq, dkv, total = pl.pallas_call(
+        functools.partial(kernel, n, pairs, rows),
         out_shape=(
             jax.ShapeDtypeStruct((heads, strips, wide, depth), jnp.float32),
             jax.ShapeDtypeStruct((heads, 2, rows, depth), jnp.float32),
+            jax.ShapeDtypeStruct((8, 128), jnp.float32),
         ),
-        in_specs=[vmem] * 5,
-        out_specs=(vmem, vmem),
+        in_specs=[vmem] * 6,
+        out_specs=(vmem, vmem, vmem),
         scratch_shapes=[
             pltpu.VMEM((heads, 2, span, depth), jnp.bfloat16),
             pltpu.VMEM((heads, hops, 2, rows, depth), jnp.bfloat16),
@@ -224,17 +374,22 @@
             pltpu.VMEM((hops, 8, rows), jnp.int32),
             pltpu.VMEM((strips, WINDOW + STRIP, wide), jnp.float32),
             pltpu.VMEM((2, span, depth), jnp.float32),
+            pltpu.VMEM((rounds + 1, 8, 128), jnp.float32),
+            pltpu.VMEM((rounds, 8, 128), jnp.float32),
             pltpu.SemaphoreType.DMA((hops,)),
             pltpu.SemaphoreType.DMA((hops,)),
             pltpu.SemaphoreType.DMA((heads, hops)),
             pltpu.SemaphoreType.DMA((heads, hops)),
             pltpu.SemaphoreType.DMA((heads, hops)),
             pltpu.SemaphoreType.DMA((heads, hops)),
+            pltpu.SemaphoreType.DMA((rounds,)),
+            pltpu.SemaphoreType.DMA((rounds,)),
         ],
         compiler_params=pltpu.CompilerParams(
             collective_id=0, has_side_effects=True, vmem_limit_bytes=56 << 20
         ),
-    )(q, g, kv, mark, own_low)
+    )(q, g, kv, mark, own_low, count)
+    factor = rows * n * pairs / total[0, 0]
     d_q = (dq * (factor * SCALE)).astype(jnp.bfloat16)
     d_q = d_q.reshape(heads, strips, group, STRIP, depth).transpose(1, 3, 0, 2, 4)
     d_queries = d_q.reshape(1, rows, heads_q, depth)

time: 227 us -> 132 us (0.58); the launches traced: 227 us -> 129 us
  Pallas kernels: 179 us -> 108 us
  blocking collectives: 30 us -> 0 us
    pallas_call x1, Pallas kernels: 179 us -> 108 us  [on_device(): pl.pallas_call(functools.partial(kernel, n, pairs, rows), out_shape=(jax....]
    psum x1 -> x0, blocking collectives: 30 us -> none  [on_device(): count_all = lax.psum(jnp.sum(loss_mask).astype(jnp.float32), ('ctx', 'dp'))]
    unnamed x14 -> x12, local copies, waits for them, and re-layouts: 4.61 us -> 4.6 us
where the time goes in v2:
time: 132 us; the launch traced here: 129 us
  Pallas kernels  108 us (82%)
  local copies, waits for them, and re-layouts  11.7 us (9%)
  other arithmetic  7.27 us (6%)
  between operations  2.05 us (2%)
    pallas_call x1, Pallas kernels, on_device(): pl.pallas_call(functools.partial(kernel, n, pairs, rows), out_shape=(jax....  108 us
    unnamed x12, local copies, waits for them, and re-layouts  4.6 us

profile of v2, /device:TPU:0, one launch (start us, length us, event | category | flops | bytes accessed | tf_op | source)
XLA Modules:
  0.0 129.3 jit_solution(304549862518936052)
XLA Ops:
  0.6 1.3 %reduce_sum.19 = s32[]{:T(128)} reduce(s32[1,256]{1,0:T(1,128)} %param.10, s32[]{:T(128)} %constant.1.clone.1), dimensions={0,1}, to_apply=%region_1.0 | reduce | flops 255 | bytes 1032 | tf_op jit(solution)/shard_map/reduce_sum | solution.py:345
  2.6 0.7 convert_reduce_fusion.1
  3.3 0.9 convert_reduce_fusion
  4.3 0.6 broadcast_in_dim.33.count_ref
  4.9 1.3 broadcast_in_dim.28.mark_ref
  6.1 0.6 broadcast_in_dim.32.low_ref
  6.7 0.0 copy-start.1
  6.7 1.2 copy.18
  7.9 1.1 copy.19
  9.1 0.0 copy-start.2
  9.1 1.1 maximum_bitcast_fusion.kv_ref
  10.2 0.0 copy-done.1
  10.2 1.2 copy_multiply_fusion
  11.4 0.0 copy-done.2
  11.4 1.3 copy.16
  12.7 108.2 %shard_map.85 = (f32[8,2,256,128]{3,2,1,0:T(8,128)}, f32[8,2,256,128]{3,2,1,0:T(8,128)}, f32[8,128]{1,0:T(8,128)}) custom-call(bf16[8,2,256,128]{3,2,1,0:T(8,128)(2,1)} %bitcast.37, bf16[8,2,256,128]{3,2,1,0:T(8,128)(2,1)} %bitcast.35, bf16[8,2,256,128]{3,2,1,0:T(8,128)(2,1)} %maximum_bitcast_fusion.kv_ref, s32[8,256]{1,0:T(8,128)} %broadcast_in_dim.28.mark_ref, ...), custom_call_target="tpu_custom_call" | custom-call | tf_op jit(solution)/shard_map/pallas_call | solution.py:361
  120.9 0.0 copy-start
  120.9 1.3 %slice.9 = f32[1,1]{1,0:T(1,128)} slice(f32[8,128]{1,0:T(8,128)} %get-tuple-element.7), slice={[0:1], [0:1]} | slice | bytes 8 | tf_op jit(solution)/shard_map/slice | solution.py:392
  122.9 1.8 %multiply_convert_fusion = bf16[8,2,256,128]{3,2,1,0:T(8,128)(2,1)S(1)} fusion(f32[8,2,256,128]{3,2,1,0:T(8,128)} %get-tuple-element.6, f32[]{:T(128)S(6)} %mul.35), kind=kLoop, calls=%fused_computation | loop fusion | flops 1048576 | bytes 3145732 | tf_op jit(solution)/shard_map/convert_element_type | solution.py:393
  124.7 0.0 copy-done
  124.8 0.2 fusion.1
  124.9 1.1 copy.22
  126.1 2.0 %copy.20 = bf16[2,128,8,2,128]{4,3,2,1,0:T(2,128)(2,1)} copy(bf16[2,128,8,2,128]{4,1,3,0,2:T(8,128)(2,1)S(1)} %bitcast.36) | data formatting | bytes 2097152 | tf_op jit(solution)/shard_map/transpose | solution.py:394
  128.1 1.1 copy.21
  (2 shorter events, 0.0 us)
Async XLA Ops:
  6.7 3.4 %copy-start.1 = (bf16[1,256,16,128]{3,2,1,0:T(8,128)(2,1)S(1)}, bf16[1,256,16,128]{3,2,1,0:T(8,128)(2,1)}, u32[]{:S(2)}) copy-start(bf16[1,256,16,128]{3,2,1,0:T(8,128)(2,1)} %param.9) | copy-start | bytes 3145732
  9.1 2.3 %copy-start.2 = (bf16[1,256,16,128]{3,2,1,0:T(8,128)(2,1)S(1)}, bf16[1,256,16,128]{3,2,1,0:T(8,128)(2,1)}, u32[]{:S(2)}) copy-start(bf16[1,256,16,128]{3,2,1,0:T(8,128)(2,1)} %param.6) | copy-start | bytes 3145732
  120.9 3.9 %copy-start = (f32[8,2,256,128]{3,2,1,0:T(8,128)S(1)}, f32[8,2,256,128]{3,2,1,0:T(8,128)}, u32[]{:S(2)}) copy-start(f32[8,2,256,128]{3,2,1,0:T(8,128)} %get-tuple-element.8) | copy-start | bytes 6291460

commit v3 on v2

--- a/solution.py
+++ b/solution.py
@@ -51,7 +51,7 @@
                 acc[kind, low + cut : low + span] = part[cut:]
 
 
-def fill_bias(rows, mark_ref, low_ref, marks, bias):
+def fill_bias(rows, mark_ref, marks, bias):
     hops = WINDOW // rows
     first = mark_ref[0:1, 0:1]
     before = jnp.zeros((1, 1), jnp.float32)
@@ -59,7 +59,13 @@
         earlier = jnp.where(marks[hop, 0:1, :] < first, 1.0, 0.0)
         before += jnp.sum(earlier, axis=1, keepdims=True)
     for strip in range(rows // STRIP):
-        own = low_ref[strip, 0:1, :].astype(jnp.float32)
+        turn = mark_ref[0:1, strip * STRIP : (strip + 1) * STRIP].astype(jnp.float32)
+        own = jnp.zeros((1, STRIP), jnp.float32)
+        for block in range(strip + 1):
+            keys = mark_ref[0:1, block * STRIP : (block + 1) * STRIP].astype(jnp.float32)
+            keys = jnp.transpose(jnp.broadcast_to(keys, (STRIP, STRIP)))
+            own += jnp.sum(jnp.where(keys < turn, 1.0, 0.0), axis=0, keepdims=True)
+        own = jnp.concatenate([own] * (bias.shape[2] // STRIP), axis=1)
         start = jnp.where(own > 0.0, own + WINDOW, before) - strip * STRIP
         shape = bias.shape[1:]
         row = lax.broadcasted_iota(jnp.int32, (1, shape[1]), 1) & (STRIP - 1)
@@ -70,9 +76,9 @@
 
 
 def kernel(
-    n, pairs, rows, q_ref, g_ref, kv_ref, mark_ref, low_ref, count_ref,
-    dq_ref, dkv_ref, total_ref,
-    ext, sent, back, marks, bias, acc, count, count_in,
+    n, pairs, rows, q_ref, g_ref, kv_ref, turn_ref, mask_ref,
+    dq_ref, dkv_ref,
+    ext, own, dq_raw, mark_ref, sent, back, marks, bias, acc, count, count_in,
     mark_send, mark_recv, kv_send, kv_recv, back_send, back_recv, count_send, count_recv,
 ):
     hops = WINDOW // rows
@@ -155,13 +161,15 @@
         def _():
             own_across(head).start()
 
+    mark_ref[...] = jnp.broadcast_to(turn_ref[...], mark_ref.shape)
     for d in range(1, hops + 1):
         @pl.when(me + d < n)
         def _():
             mark_copy(d).start()
     for head in range(min(AHEAD, heads)):
         send_own(head)
-    count[0] = count_ref[...]
+    ones = jnp.sum(mask_ref[...].astype(jnp.float32), axis=1, keepdims=True)
+    count[0] = jnp.broadcast_to(ones, count.shape[1:])
     count_copy(0).start()
 
     def place_own(head, carry):
@@ -184,11 +192,11 @@
         @pl.when(me >= d)
         def _():
             mark_copy(d).wait_recv()
-    fill_bias(rows, mark_ref, low_ref, marks, bias)
+    fill_bias(rows, mark_ref, marks, bias)
 
     def step(s, carry):
         for k in range(len(bits)):
-            @pl.when(s == k)
+            @pl.when(s == k // 2)
             def _():
                 count_copy(k).wait_recv()
                 count[k + 1] = count[k] + count_in[k]
@@ -229,55 +237,6 @@
             def _():
                 kv_copy(s - 1, 3).start()
 
-        @pl.when((s >= 3) & (s < heads + 3))
-        def _():
-            head = s - 3
-
-            @pl.when(me >= 1)
-            def _():
-                @pl.when(me + 2 < n)
-                def _():
-                    back_copy(head, 3).wait_recv()
-                    add_in(head, 1, 3)
-
-                back_copy(head, 1).start()
-
-            @pl.when((odd == 0) & (me >= 2))
-            def _():
-                @pl.when(me + 2 < n)
-                def _():
-                    back_copy(head, 4).wait_recv()
-                    add_in(head, 2, 4)
-
-                back_copy(head, 2).start()
-
-        @pl.when((s >= 4) & (s < heads + 4) & (odd == 1) & (me >= 2))
-        def _():
-            head = s - 4
-
-            @pl.when(me + 2 < n)
-            def _():
-                back_copy(head, 4).wait_recv()
-                add_in(head, 2, 4)
-
-            back_copy(head, 1).wait_recv()
-            add_in(head, 2, 1)
-            back_copy(head, 2).start()
-
-        @pl.when(s >= 5)
-        def _():
-            head = s - 5
-
-            @pl.when(odd == 0)
-            def _():
-                back_copy(head, 1).wait_recv()
-                dkv_ref[head] += back[head, 0].astype(jnp.float32)
-
-            @pl.when(me + 2 < n)
-            def _():
-                back_copy(head, 2).wait_recv()
-                dkv_ref[head] += back[head, 1].astype(jnp.float32)
-
         @pl.when((s >= 2) & (s < heads + 2))
         def _():
             head = s - 2
@@ -285,15 +244,72 @@
                 @pl.when(me >= d)
                 def _():
                     kv_copy(head, d).wait_recv()
-            head_grads(head, rows, q_ref, g_ref, ext, bias, acc, dq_ref)
-            for d in (4, 3, 2, 1):
+            head_grads(head, rows, q_ref, g_ref, ext, bias, acc, dq_raw)
+            for d in (3, 4, 2, 1):
                 low = WINDOW - d * rows
                 sent[head, d - 1] = acc[:, low : low + rows, :].astype(sent.dtype)
                 if d > 2:
                     @pl.when(me >= d)
                     def _():
                         back_copy(head, d).start()
-            dkv_ref[head] = acc[:, WINDOW : WINDOW + rows, :]
+            own[head] = acc[:, WINDOW : WINDOW + rows, :]
+
+        @pl.when((s >= 3) & (s < heads + 3))
+        def _():
+            head = s - 3
+
+            @pl.when(me >= 1)
+            def _():
+                @pl.when(me + 2 < n)
+                def _():
+                    back_copy(head, 3).wait_recv()
+                    add_in(head, 1, 3)
+
+                back_copy(head, 1).start()
+
+            @pl.when((odd == 0) & (me >= 2))
+            def _():
+                @pl.when(me + 2 < n)
+                def _():
+                    back_copy(head, 4).wait_recv()
+                    add_in(head, 2, 4)
+
+                back_copy(head, 2).start()
+
+        @pl.when((s >= 4) & (s < heads + 4) & (odd == 1) & (me >= 2))
+        def _():
+            head = s - 4
+
+            @pl.when(me + 2 < n)
+            def _():
+                back_copy(head, 4).wait_recv()
+                add_in(head, 2, 4)
+
+            back_copy(head, 1).wait_recv()
+            add_in(head, 2, 1)
+            back_copy(head, 2).start()
+
+        @pl.when(s >= 5)
+        def _():
+            head = s - 5
+
+            @pl.when(odd == 0)
+            def _():
+                back_copy(head, 1).wait_recv()
+                own[head] += back[head, 0].astype(jnp.float32)
+
+            @pl.when(me + 2 < n)
+            def _():
+                back_copy(head, 2).wait_recv()
+                own[head] += back[head, 1].astype(jnp.float32)
+
+            factor = (rows * n * pairs) / count[len(bits), 0:1, 0:1]
+            dkv_ref[head, 0] = (own[head, 0] * (factor * SCALE)).astype(dkv_ref.dtype)
+            dkv_ref[head, 1] = (own[head, 1] * factor).astype(dkv_ref.dtype)
+            for strip in range(rows // STRIP):
+                dq_ref[head, strip] = (
+                    dq_raw[head, strip] * (factor * SCALE)
+                ).astype(dq_ref.dtype)
 
         return carry
 
@@ -329,7 +345,6 @@
             mark_copy(d).wait_send()
     for k in range(len(bits)):
         count_copy(k).wait_send()
-    total_ref[...] = count[len(bits)]
 
 
 def on_device(queries, keys, values, d_out, loss_mask, turn_ids):
@@ -342,7 +357,6 @@
     wide = group * STRIP
     pairs = lax.axis_size("dp")
     rounds = n.bit_length() + pairs.bit_length() - 2
-    count = jnp.full((8, 128), jnp.sum(loss_mask).astype(jnp.float32))
 
     def by_strip(array):
         array = array.reshape(strips, STRIP, heads, group, depth)
@@ -351,24 +365,21 @@
     q = by_strip(queries[0])
     g = by_strip(d_out[0] * loss_mask[0][:, None, None].astype(jnp.bfloat16))
     kv = jnp.stack([keys[0], values[0]]).transpose(2, 0, 1, 3)
-    turn = turn_ids[0]
-    own_low = jnp.sum((turn[None, :] < turn[:, None]).astype(jnp.int32), axis=1)
-    own_low = own_low.reshape(strips, 1, 1, STRIP)
-    own_low = jnp.broadcast_to(own_low, (strips, 8, group, STRIP)).reshape(strips, 8, wide)
-    mark = jnp.broadcast_to(turn[None, :], (8, rows))
     vmem = pl.BlockSpec(memory_space=pltpu.VMEM)
     span = WINDOW + rows
-    dq, dkv, total = pl.pallas_call(
+    dq, dkv = pl.pallas_call(
         functools.partial(kernel, n, pairs, rows),
         out_shape=(
-            jax.ShapeDtypeStruct((heads, strips, wide, depth), jnp.float32),
-            jax.ShapeDtypeStruct((heads, 2, rows, depth), jnp.float32),
-            jax.ShapeDtypeStruct((8, 128), jnp.float32),
+            jax.ShapeDtypeStruct((heads, strips, wide, depth), jnp.bfloat16),
+            jax.ShapeDtypeStruct((heads, 2, rows, depth), jnp.bfloat16),
         ),
-        in_specs=[vmem] * 6,
-        out_specs=(vmem, vmem, vmem),
+        in_specs=[vmem] * 5,
+        out_specs=(vmem, vmem),
         scratch_shapes=[
             pltpu.VMEM((heads, 2, span, depth), jnp.bfloat16),
+            pltpu.VMEM((heads, 2, rows, depth), jnp.float32),
+            pltpu.VMEM((heads, strips, wide, depth), jnp.float32),
+            pltpu.VMEM((8, rows), jnp.int32),
             pltpu.VMEM((heads, hops, 2, rows, depth), jnp.bfloat16),
             pltpu.VMEM((heads, hops, 2, rows, depth), jnp.bfloat16),
             pltpu.VMEM((hops, 8, rows), jnp.int32),
@@ -388,13 +399,11 @@
         compiler_params=pltpu.CompilerParams(
             collective_id=0, has_side_effects=True, vmem_limit_bytes=56 << 20
         ),
-    )(q, g, kv, mark, own_low, count)
-    factor = rows * n * pairs / total[0, 0]
-    d_q = (dq * (factor * SCALE)).astype(jnp.bfloat16)
-    d_q = d_q.reshape(heads, strips, group, STRIP, depth).transpose(1, 3, 0, 2, 4)
-    d_queries = d_q.reshape(1, rows, heads_q, depth)
-    d_keys = (dkv[:, 0] * (factor * SCALE)).astype(jnp.bfloat16).transpose(1, 0, 2)[None]
-    d_values = (dkv[:, 1] * factor).astype(jnp.bfloat16).transpose(1, 0, 2)[None]
+    )(q, g, kv, turn_ids, loss_mask)
+    dq = dq.reshape(heads, strips, group, STRIP, depth).transpose(1, 3, 0, 2, 4)
+    d_queries = dq.reshape(1, rows, heads_q, depth)
+    d_keys = dkv[:, 0].transpose(1, 0, 2)[None]
+    d_values = dkv[:, 1].transpose(1, 0, 2)[None]
     return (d_queries, d_keys, d_values)
 
 

time: 132 us -> 120 us (0.909); the launches traced: 129 us -> 119 us
  other arithmetic: 7.27 us -> 2.33 us
  local copies, waits for them, and re-layouts: 11.7 us -> 9.55 us
  between operations: 2.05 us -> 0.68 us
    broadcast_in_dim x3 -> x1, local copies, waits for them, and re-layouts: 2.48 us -> 0.07 us  [on_device(): d_values = dkv[:, 1].transpose(1, 0, 2)[None]]
    reduce_sum x2 -> x0, other arithmetic: 2.25 us -> none  [the longest x1 1.32 us: on_device(): count = jnp.full((8, 128), jnp.sum(loss_mask).astype(jnp.float32))]
    convert_element_type x1 -> x0, other arithmetic: 1.83 us -> none  [on_device(): d_q = (dq * (factor * SCALE)).astype(jnp.bfloat16)]
    pallas_call x1, Pallas kernels: 108 us -> 107 us  [on_device(): pl.pallas_call(functools.partial(kernel, n, pairs, rows), out_shape=(jax....]
    slice x1 -> x0, local copies, waits for them, and re-layouts: 1.33 us -> none  [on_device(): factor = rows * n * pairs / total[0, 0]]
    unnamed x12 -> x14, local copies, waits for them, and re-layouts: 4.6 us -> 4.87 us
where the time goes in v3:
time: 120 us; the launch traced here: 119 us
  Pallas kernels  107 us (89%)
  local copies, waits for them, and re-layouts  9.55 us (8%)
  other arithmetic  2.33 us (2%)
    pallas_call x1, Pallas kernels, on_device(): pl.pallas_call(functools.partial(kernel, n, pairs, rows), out_shape=(jax....  107 us
    unnamed x14, local copies, waits for them, and re-layouts  4.87 us
    transpose x1, local copies, waits for them, and re-layouts, on_device(): dq = dq.reshape(heads, strips, group, STRIP, depth).transpose(1, 3, 0, 2, 4)  3.36 us

profile of v3, /device:TPU:0, one launch (start us, length us, event | category | flops | bytes accessed | tf_op | source)
XLA Modules:
  0.0 119.3 jit_solution(7854278538064823747)
XLA Ops:
  0.6 0.0 copy-start.4
  0.6 0.7 copy-done.4
  1.3 0.0 copy-start.3
  1.3 1.2 copy.11
  2.5 0.0 copy-done.3
  2.5 0.1 copy.12
  2.6 0.0 copy-start
  2.6 1.1 maximum_bitcast_fusion.kv_ref
  3.7 0.5 copy-done
  4.2 0.0 copy-start.1
  4.2 1.2 %copy_multiply_fusion = bf16[2,128,8,2,128]{4,1,3,0,2:T(8,128)(2,1)} fusion(bf16[2,128,8,2,128]{4,3,2,1,0:T(2,128)(2,1)S(1)} %bitcast.29, bf16[2,128]{1,0:T(2,128)(2,1)S(1)} %bitcast.33), kind=kLoop, calls=%fused_computation.1 | loop fusion | flops 524288 | bytes 2097664 | tf_op jit(solution)/shard_map/mul | solution.py:366
  5.4 0.2 copy-done.1
  5.6 1.3 %copy.9 = bf16[2,128,8,2,128]{4,1,3,0,2:T(8,128)(2,1)} copy(bf16[2,128,8,2,128]{4,3,2,1,0:T(2,128)(2,1)S(1)} %bitcast.30) | data formatting | bytes 2097152 | tf_op jit(solution)/shard_map/reshape;squeeze | solution.py:362
  6.8 106.7 %shard_map.85 = (bf16[8,2,256,128]{3,2,1,0:T(8,128)(2,1)}, bf16[8,2,256,128]{3,2,1,0:T(8,128)(2,1)}) custom-call(bf16[8,2,256,128]{3,2,1,0:T(8,128)(2,1)} %bitcast.28, bf16[8,2,256,128]{3,2,1,0:T(8,128)(2,1)} %bitcast.27, bf16[8,2,256,128]{3,2,1,0:T(8,128)(2,1)} %maximum_bitcast_fusion.kv_ref, s32[1,256]{1,0:T(1,128)} %turn_ref.1, s32[1,256]{1,0:T(1,128)} %mask_ref.1), custom_call_target="tpu_custom_call" | custom-call | tf_op jit(solution)/shard_map/pallas_call | solution.py:370
  113.5 0.0 copy-start.2
  113.5 3.4 %copy.13 = bf16[2,128,8,2,128]{4,3,2,1,0:T(2,128)(2,1)} copy(bf16[2,128,8,2,128]{4,1,3,0,2:T(8,128)(2,1)} %bitcast.32) | data formatting | bytes 2097152 | tf_op jit(solution)/shard_map/transpose | solution.py:403
  116.9 0.0 copy-done.2
  116.9 0.1 slice_bitcast_fusion
  117.0 1.1 copy.15
  118.1 1.1 copy.14
  (1 shorter events, 0.0 us)
Async XLA Ops:
  0.6 0.7 copy-start.4
  1.3 1.2 %copy-start.3 = (bf16[1,256,8,128]{3,2,1,0:T(8,128)(2,1)S(1)}, bf16[1,256,8,128]{3,2,1,0:T(8,128)(2,1)}, u32[]{:S(2)}) copy-start(bf16[1,256,8,128]{3,2,1,0:T(8,128)(2,1)} %param.8) | copy-start | bytes 1572868
  2.6 1.6 %copy-start = (bf16[1,256,16,128]{3,2,1,0:T(8,128)(2,1)S(1)}, bf16[1,256,16,128]{3,2,1,0:T(8,128)(2,1)}, u32[]{:S(2)}) copy-start(bf16[1,256,16,128]{3,2,1,0:T(8,128)(2,1)} %param.9) | copy-start | bytes 3145732
  4.2 1.4 %copy-start.1 = (bf16[1,256,16,128]{3,2,1,0:T(8,128)(2,1)S(1)}, bf16[1,256,16,128]{3,2,1,0:T(8,128)(2,1)}, u32[]{:S(2)}) copy-start(bf16[1,256,16,128]{3,2,1,0:T(8,128)(2,1)} %param.6) | copy-start | bytes 3145732
  113.5 3.4 %copy-start.2 = (bf16[8,2,256,128]{3,2,1,0:T(8,128)(2,1)S(1)}, bf16[8,2,256,128]{3,2,1,0:T(8,128)(2,1)}, u32[]{:S(2)}) copy-start(bf16[8,2,256,128]{3,2,1,0:T(8,128)(2,1)} %get-tuple-element.6) | copy-start | bytes 3145732
